TPU v7x, 32 devices: a whole 2x2x4 slice. The times are simulated.
32 devices in a mesh: node: 8 (over z, y), rep: 4 (over x, core).
Axes of the slice: x: 2, y: 2, z: 4, core: 2. Of those that a mesh axis runs over, the one named last changes fastest.
Arguments:
- features: bfloat16 [16384, 256], P('node'), may hold values from -6 to 6
- tiles: bfloat16 [8, 4, 4, 96, 128, 128], P('node', 'rep'), may hold values from -0.09375 to 0.09375
- tile_rows: int32 [8, 4, 4, 96], P('node', 'rep'), may hold values from 0 to 15
- tile_cols: int32 [8, 4, 4, 96], P('node', 'rep'), may hold values from 0 to 15
- tile_count: int32 [8, 4, 4], P('node', 'rep'), may hold values from 1 to 96, as said below
- order: int32 [16384], P('node'), may hold values from 0 to 16383, as said below
- weight: bfloat16 [256, 256], replicated, may hold values from -0.375 to 0.375
- cotangent: bfloat16 [16384, 256], P(('node', 'rep')), may hold values from -6 to 6
Outputs:
- activated: bfloat16 [16384, 256], P(('node', 'rep'))
- feature_grad: bfloat16 [16384, 256], P(('node', 'rep'))
- weight_grad: float32 [256, 256], replicated
Inputs may be any that keep to these rules, and one draw needn't show every extreme that they name: `tile_count`: for every node block and offset, exactly one tile group holds 96 live slots; the counts of the others lie between 1 and 32. order is a permutation of the nodes that maps each aligned block of 512 positions onto itself.
All inputs are finite; a program needn't handle non-finite values.
Results may differ from a plain program's by a relative error of at most 0.017.
Values may be sent and summed in bfloat16 or wider, within the bound.
A program may use at most 128 MiB of HBM per device.

v0:
```python
import functools
import math

import jax
import jax.numpy as jnp
from jax import lax
from jax.experimental import pallas as pl
from jax.experimental.pallas import tpu as pltpu
from jax.sharding import PartitionSpec as P

CHUNK = 8
GROUP = 4


def stream(tiles, held, sems, count_ref, ks, step):
    chunks = tiles.shape[1] // CHUNK

    def copy(j, c):
        return pltpu.make_async_copy(
            tiles.at[ks[j], pl.ds(c * CHUNK, CHUNK)],
            held.at[j, pl.ds(c * CHUNK, CHUNK)],
            sems.at[j * chunks + c],
        )

    for j, k in enumerate(ks):
        live = lax.div(count_ref[k] + (CHUNK - 1), CHUNK)

        def begin(c, _, j=j):
            copy(j, c).start()
            return 0

        lax.fori_loop(0, live, begin, 0)
    for j, k in enumerate(ks):
        before, body, after = step(j, k)
        before()
        full = lax.div(count_ref[k], CHUNK)
        rest = count_ref[k] - full * CHUNK

        def whole(c, _, j=j):
            copy(j, c).wait()
            for g in range(0, CHUNK, GROUP):
                body([c * CHUNK + g + i for i in range(GROUP)])
            return 0

        lax.fori_loop(0, full, whole, 0)

        @pl.when(rest > 0)
        def _(j=j):
            copy(j, full).wait()

            def one(s, _):
                body([full * CHUNK + s])
                return 0

            lax.fori_loop(0, rest, one, 0)

        after()


def forward_kernel(ks, capacity, seeded, *refs):
    if seeded:
        count_ref, row_ref, col_ref, tiles, source, seed, out, held, acc, sems = refs
    else:
        count_ref, row_ref, col_ref, tiles, source, out, held, acc, sems = refs
    per = source.shape[2]
    if seeded:
        acc[...] = seed[...]
    else:
        acc[...] = jnp.zeros_like(acc)

    def step(j, k):
        def body(slots):
            products, puts = [], []
            for s in slots:
                col = col_ref[k * capacity + s]
                puts.append(row_ref[k * capacity + s])
                products.append(
                    jnp.dot(
                        held[j, s],
                        source[lax.div(col, per), j, lax.rem(col, per)],
                        preferred_element_type=jnp.float32,
                    )
                )
            for put, product in zip(puts, products):
                acc[put] += product

        return (lambda: None), body, (lambda: None)

    stream(tiles, held, sems, count_ref, ks, step)
    out[...] = acc[...].astype(out.dtype)


def backward_kernel(ks, capacity, count_ref, row_ref, col_ref, tiles, source, out, held, acc, sems):
    per = out.shape[2]

    def step(j, k):
        def before():
            acc[...] = jnp.zeros_like(acc)

        def body(slots):
            products, puts = [], []
            for s in slots:
                puts.append(col_ref[k * capacity + s])
                products.append(
                    lax.dot_general(
                        held[j, s],
                        source[row_ref[k * capacity + s]],
                        (((0,), (0,)), ((), ())),
                        preferred_element_type=jnp.float32,
                    )
                )
            for put, product in zip(puts, products):
                acc[put] += product

        def after():
            for q in range(out.shape[0]):
                out[q, j] = acc[q * per : (q + 1) * per].astype(out.dtype)

        return before, body, after

    stream(tiles, held, sems, count_ref, ks, step)


def tile_call(kernel, ks, out_shape, out_dtype, acc_shape, args, tiles):
    capacity, size = tiles.shape[1], tiles.shape[-1]
    smem = pl.BlockSpec(memory_space=pltpu.SMEM)
    vmem = pl.BlockSpec(memory_space=pltpu.VMEM)
    return pl.pallas_call(
        kernel,
        out_shape=jax.ShapeDtypeStruct(out_shape, out_dtype),
        in_specs=[smem] * 3 + [pl.BlockSpec(memory_space=pl.ANY)] + [vmem] * (len(args) - 4),
        out_specs=vmem,
        scratch_shapes=[
            pltpu.VMEM((len(ks), capacity, size, size), tiles.dtype),
            pltpu.VMEM(acc_shape, jnp.float32),
            pltpu.SemaphoreType.DMA((len(ks) * (capacity // CHUNK),)),
        ],
        compiler_params=pltpu.CompilerParams(vmem_limit_bytes=60 * 1024 * 1024),
    )(*args)


def hop(src, dst, send, recv, axis, target):
    copy = pltpu.make_async_remote_copy(
        src_ref=src,
        dst_ref=dst,
        send_sem=send,
        recv_sem=recv,
        device_id={axis: target},
        device_id_type=pl.DeviceIdType.MESH,
    )
    copy.start()
    return copy


def greet(peers):
    barrier = pltpu.get_barrier_semaphore()
    for axis, target in peers:
        pl.semaphore_signal(
            barrier, inc=1, device_id={axis: target}, device_id_type=pl.DeviceIdType.MESH
        )
    pl.semaphore_wait(barrier, len(peers))


def dense_kernel(part, cot, weight, act, wpart, back, near, outgoing, far, full, send, recv):
    me = lax.axis_index("rep")
    x, c = me // 2, me % 2
    ox, oc = 1 - x, 1 - c
    sib, across, diag = x * 2 + oc, ox * 2 + c, ox * 2 + oc
    greet([("rep", sib), ("rep", across)])
    first = hop(part.at[diag], near.at[0], send.at[0], recv.at[0], "rep", sib)
    second = hop(part.at[sib], near.at[1], send.at[1], recv.at[1], "rep", sib)
    first.wait()
    outgoing[...] = (part[across].astype(jnp.float32) + near[0].astype(jnp.float32)).astype(
        outgoing.dtype
    )
    third = hop(outgoing, far, send.at[2], recv.at[2], "rep", across)
    second.wait()
    mine = part[me].astype(jnp.float32) + near[1].astype(jnp.float32)
    third.wait()
    aggregate = (mine + far[...].astype(jnp.float32)).astype(jnp.bfloat16)
    pre_act = jnp.dot(aggregate, weight[...], preferred_element_type=jnp.float32)
    gate = jax.nn.sigmoid(pre_act)
    act[...] = (pre_act * gate).astype(act.dtype)
    pre_grad = (
        cot[...].astype(jnp.float32) * gate * (1.0 + pre_act * (1.0 - gate))
    ).astype(jnp.bfloat16)
    full[me] = lax.dot_general(
        pre_grad, weight[...], (((1,), (1,)), ((), ())), preferred_element_type=jnp.float32
    ).astype(full.dtype)
    over = hop(full.at[me], full.at[me], send.at[3], recv.at[3], "rep", across)
    side = hop(full.at[me], full.at[me], send.at[4], recv.at[4], "rep", sib)
    wpart[...] = lax.dot_general(
        aggregate, pre_grad, (((0,), (0,)), ((), ())), preferred_element_type=jnp.float32
    )
    over.wait()
    relay = hop(full.at[across], full.at[across], send.at[5], recv.at[5], "rep", sib)
    side.wait()
    relay.wait()
    back[...] = full[...]


def halo_kernel(nodes, mine, out, full, send, recv):
    me, here = lax.axis_index("rep"), lax.axis_index("node")
    x, c = me // 2, me % 2
    sib, across = x * 2 + 1 - c, (1 - x) * 2 + c
    greet(
        [("rep", sib), ("rep", across)]
        + [("node", (here + d) % nodes) for d in (1, nodes - 1, 2, nodes - 2)]
    )
    arrivals = [
        hop(mine, full.at[me, j], send.at[j], recv.at[j], "node", (here + d) % nodes)
        for j, d in enumerate((nodes - 1, 1, 2))
    ]
    over, rest = [], []
    for j in range(3):
        arrivals[j].wait()
        own = full.at[me, j]
        over.append(hop(own, own, send.at[3 + j], recv.at[3 + j], "rep", across))
        rest.append(hop(own, own, send.at[6 + j], recv.at[6 + j], "rep", sib))
    for j in range(3):
        over[j].wait()
        other = full.at[across, j]
        rest.append(hop(other, other, send.at[9 + j], recv.at[9 + j], "rep", sib))
    for copy in rest:
        copy.wait()
    out[...] = full[...]


def halo_call(mine, reps):
    shape = (reps, 3) + mine.shape
    vmem = pl.BlockSpec(memory_space=pltpu.VMEM)
    return pl.pallas_call(
        functools.partial(halo_kernel, lax.axis_size("node")),
        out_shape=jax.ShapeDtypeStruct(shape, mine.dtype),
        in_specs=[vmem],
        out_specs=vmem,
        scratch_shapes=[
            pltpu.VMEM(shape, mine.dtype),
            pltpu.SemaphoreType.DMA((12,)),
            pltpu.SemaphoreType.DMA((12,)),
        ],
        compiler_params=comm_params(2),
    )(mine)


def finish_kernel(
    nodes, reps, scale, terms, pick, part, grad, out,
    near, outgoing, far, leaving, got, total, from_rep, held, from_node, full,
    send, recv, rs, rr, ns, nr, gs, gr, os, orr,
):
    me, here = lax.axis_index("rep"), lax.axis_index("node")
    x, c = me // 2, me % 2
    sib, across, diag = x * 2 + 1 - c, (1 - x) * 2 + c, (1 - x) * 2 + 1 - c
    rep_peers = [(me + d) % reps for d in range(1, reps)]
    node_peers = [(here + d) % nodes for d in range(1, nodes)]
    greet([("rep", p) for p in rep_peers] + [("node", p) for p in node_peers])
    first = [
        hop(terms.at[diag, j], near.at[0, j], send.at[j], recv.at[j], "rep", sib)
        for j in range(4)
    ]
    second = [
        hop(terms.at[sib, j], near.at[1, j], send.at[4 + j], recv.at[4 + j], "rep", sib)
        for j in range(4)
    ]
    to_reps = [
        hop(part.at[p], from_rep.at[i], rs.at[i], rr.at[i], "rep", p)
        for i, p in enumerate(rep_peers)
    ]
    third = []
    for j in range(4):
        first[j].wait()
        outgoing[j] = (
            terms[across, j].astype(jnp.float32) + near[0, j].astype(jnp.float32)
        ).astype(outgoing.dtype)
        third.append(hop(outgoing.at[j], far.at[j], send.at[8 + j], recv.at[8 + j], "rep", across))
    for copy in to_reps:
        copy.wait()
    share = part[me]
    for i in range(reps - 1):
        share = share + from_rep[i]
    held[...] = share
    to_nodes = [
        hop(held.at[p], from_node.at[i], ns.at[i], nr.at[i], "node", p)
        for i, p in enumerate(node_peers)
    ]
    fourth = []
    for j, d in enumerate((1, nodes - 1, nodes - 2, 0)):
        second[j].wait()
        third[j].wait()
        value = (
            terms[me, j].astype(jnp.float32)
            + near[1, j].astype(jnp.float32)
            + far[j].astype(jnp.float32)
        )
        if d:
            leaving[j] = value.astype(leaving.dtype)
            fourth.append(
                hop(leaving.at[j], got.at[j], send.at[12 + j], recv.at[12 + j], "node", (here + d) % nodes)
            )
        else:
            total[...] = value
    for copy in to_nodes:
        copy.wait()
    share = held[here]
    for i in range(nodes - 1):
        share = share + from_node[i]
    full[me, here] = share * scale
    spread = [
        hop(full.at[me, here], full.at[me, here], gs.at[i], gr.at[i], "node", p)
        for i, p in enumerate(node_peers)
    ]
    for copy in spread:
        copy.wait()
    gather = [
        hop(full.at[me], full.at[me], os.at[i], orr.at[i], "rep", p)
        for i, p in enumerate(rep_peers)
    ]
    for copy in fourth:
        copy.wait()
    value = total[...]
    for j in range(3):
        value = value + got[j].astype(jnp.float32)
    grad[...] = lax.dot_general(
        pick[...], value.astype(jnp.bfloat16), (((0,), (0,)), ((), ())), preferred_element_type=jnp.float32
    ).astype(grad.dtype)
    for copy in gather:
        copy.wait()
    out[...] = full[...]


def finish_call(terms, pick, part, scale):
    nodes, reps = lax.axis_size("node"), lax.axis_size("rep")
    rows = part.size // (nodes * reps * 128)
    shape = (reps, nodes, rows, 128)
    block = terms.shape[2:]
    vmem = pl.BlockSpec(memory_space=pltpu.VMEM)
    sems = [
        pltpu.SemaphoreType.DMA((n,))
        for n in (15, 15) + (reps - 1,) * 2 + (nodes - 1,) * 4 + (reps - 1,) * 2
    ]
    grad, out = pl.pallas_call(
        functools.partial(finish_kernel, nodes, reps, scale),
        out_shape=(
            jax.ShapeDtypeStruct(block, jnp.bfloat16),
            jax.ShapeDtypeStruct(shape, jnp.float32),
        ),
        in_specs=[vmem] * 3,
        out_specs=(vmem,) * 2,
        scratch_shapes=[
            pltpu.VMEM((2, 4) + block, jnp.bfloat16),
            pltpu.VMEM((4,) + block, jnp.bfloat16),
            pltpu.VMEM((4,) + block, jnp.bfloat16),
            pltpu.VMEM((3,) + block, jnp.bfloat16),
            pltpu.VMEM((3,) + block, jnp.bfloat16),
            pltpu.VMEM(block, jnp.float32),
            pltpu.VMEM((reps - 1, nodes, rows, 128), jnp.float32),
            pltpu.VMEM((nodes, rows, 128), jnp.float32),
            pltpu.VMEM((nodes - 1, rows, 128), jnp.float32),
            pltpu.VMEM(shape, jnp.float32),
        ]
        + sems,
        compiler_params=comm_params(1),
    )(terms, pick, part.reshape(shape))
    return grad, out.reshape(part.shape)


def comm_params(ident):
    return pltpu.CompilerParams(
        collective_id=ident, has_side_effects=True, vmem_limit_bytes=60 * 1024 * 1024
    )


def dense_call(part, cot, weight):
    reps, rows, feat = part.shape
    vmem = pl.BlockSpec(memory_space=pltpu.VMEM)
    half = (rows, feat)
    return pl.pallas_call(
        dense_kernel,
        out_shape=(
            jax.ShapeDtypeStruct(half, jnp.bfloat16),
            jax.ShapeDtypeStruct((feat, feat), jnp.float32),
            jax.ShapeDtypeStruct(part.shape, jnp.bfloat16),
        ),
        in_specs=[vmem] * 3,
        out_specs=(vmem,) * 3,
        scratch_shapes=[
            pltpu.VMEM((2,) + half, jnp.bfloat16),
            pltpu.VMEM(half, jnp.bfloat16),
            pltpu.VMEM(half, jnp.bfloat16),
            pltpu.VMEM(part.shape, jnp.bfloat16),
            pltpu.SemaphoreType.DMA((6,)),
            pltpu.SemaphoreType.DMA((6,)),
        ],
        compiler_params=comm_params(0),
    )(part, cot, weight)


def local(features, tiles, tile_rows, tile_cols, tile_count, order, weight, cotangent):
    rows_dev, feat = features.shape
    size = tiles.shape[-1]
    blocks = rows_dev // size
    quarter = cotangent.shape[0]
    reps = lax.axis_size("rep")
    per = blocks // reps
    rep_pos = lax.axis_index("rep")
    tile_set = tiles[0, 0]
    capacity = tile_set.shape[1]
    row_ids = tile_rows.reshape(-1)
    col_ids = tile_cols.reshape(-1)
    counts = tile_count.reshape(-1)

    within = (order % quarter).reshape(reps, quarter)
    spots = jnp.arange(quarter, dtype=jnp.int32)
    my_order = lax.dynamic_index_in_dim(within, rep_pos, 0, keepdims=False)
    my_pick = (my_order[:, None] == spots[None, :]).astype(jnp.bfloat16)
    my_features = lax.dynamic_slice_in_dim(features, rep_pos * quarter, quarter, 0)
    mine = jnp.dot(my_pick, my_features, preferred_element_type=jnp.float32).astype(jnp.bfloat16)
    gathered = halo_call(mine, reps)
    gathered = gathered.reshape(reps, 3, per, size, feat)

    pick = (within[:, :, None] == spots[None, None, :]).astype(jnp.bfloat16)
    here = jnp.einsum(
        "qpi,qif->qpf",
        pick,
        features.reshape(reps, quarter, feat),
        preferred_element_type=jnp.float32,
    ).astype(jnp.bfloat16)
    here = here.reshape(reps, 1, per, size, feat)

    acc_shape = (blocks, size, feat)
    scalars = (counts, row_ids, col_ids, tile_set)
    own = tile_call(
        functools.partial(forward_kernel, (1,), capacity, False),
        (1,), acc_shape, jnp.float32, acc_shape, scalars + (here,), tile_set,
    )
    partial_value = tile_call(
        functools.partial(forward_kernel, (0, 2, 3), capacity, True),
        (0, 2, 3), acc_shape, jnp.bfloat16, acc_shape, scalars + (gathered, own), tile_set,
    )
    activated, weight_part, full_back = dense_call(
        partial_value.reshape(reps, quarter, feat), cotangent, weight
    )
    full_back = full_back.reshape(blocks, size, feat)
    grad_scale = 1.0 / math.sqrt(rows_dev * lax.axis_size("node"))
    terms = tile_call(
        functools.partial(backward_kernel, (0, 2, 3, 1), capacity),
        (0, 2, 3, 1), (reps, 4, per, size, feat), jnp.bfloat16, acc_shape, scalars + (full_back,), tile_set,
    )
    feature_grad, weight_grad = finish_call(
        terms.reshape(reps, 4, quarter, feat), my_pick, weight_part, grad_scale
    )
    return (activated, feature_grad, weight_grad)


def solution(mesh):
    placed = (
        P("node", None),
        P("node", "rep", None, None, None, None),
        P("node", "rep", None, None),
        P("node", "rep", None, None),
        P("node", "rep", None),
        P("node"),
        P(),
        P(("node", "rep"), None),
    )
    return jax.shard_map(
        local,
        mesh=mesh,
        in_specs=placed,
        out_specs=(P(("node", "rep"), None), P(("node", "rep"), None), P()),
        check_vma=False,
    )
```

profile of v0, /device:TPU:0, one launch (start us, length us, event | category | flops | bytes accessed | tf_op | source)
XLA Modules:
  0.0 153.0 jit_solution(10950567124677012623)
XLA Ops:
  0.6 0.0 copy-start
  0.6 0.0 copy-start.3
  0.7 0.0 copy-start.4
  0.7 0.8 add_select_fusion
  1.5 0.4 copy-done
  1.9 1.1 convolution_convert_fusion.mine
  2.9 41.2 %shard_map.103 = bf16[4,3,512,256]{3,2,1,0:T(8,128)(2,1)} custom-call(bf16[512,256]{1,0:T(8,128)(2,1)} %convolution_convert_fusion.mine), custom_call_target="tpu_custom_call" | custom-call | tf_op jit(solution)/shard_map/pallas_call | solution.py:232
  44.2 0.0 copy-done.3
  44.2 0.7 reshape.46.refs_1_.row_ref
  44.8 0.0 copy-done.4
  44.8 0.7 reshape.47.refs_2_.col_ref
  45.5 1.8 %fusion.2 = bf16[4,512,256]{2,1,0:T(8,128)(2,1)} fusion(bf16[4,512,256]{2,1,0:T(8,128)(2,1)S(1)} %bitcast.12, s32[4,512]{1,0:T(4,128)S(1)} %reshape.48), kind=kOutput, calls=%fused_computation.3 | convolution fusion | flops 538443776 | bytes 2105344 | tf_op jit(solution)/shard_map/qpi,qif->qpf/dot_general | solution.py:422
  47.3 4.8 %shard_map.104.refs_5_ = f32[16,128,256]{2,1,0:T(8,128)} custom-call(s32[4]{0:T(128)} %bitcast.23, s32[384]{0:T(512)} %reshape.46.refs_1_.row_ref, s32[384]{0:T(512)} %reshape.47.refs_2_.col_ref, bf16[4,96,128,128]{3,2,1,0:T(8,128)(2,1)} %bitcast.13, bf16[4,1,4,128,256]{4,3,2,1,0:T(8,128)(2,1)} %bitcast.20), custom_call_target="tpu_custom_call" | custom-call | tf_op jit(solution)/shard_map/pallas_call | solution.py:128
  52.2 8.6 %shard_map.105 = bf16[16,128,256]{2,1,0:T(8,128)(2,1)} custom-call(s32[4]{0:T(128)} %bitcast.24, s32[384]{0:T(512)} %reshape.46.refs_1_.row_ref, s32[384]{0:T(512)} %reshape.47.refs_2_.col_ref, bf16[4,96,128,128]{3,2,1,0:T(8,128)(2,1)} %bitcast.14, bf16[4,3,4,128,256]{4,3,2,1,0:T(8,128)(2,1)} %bitcast.17, f32[16,128,256]{2,1,0:T(8,128)} %shard_map.104.refs_5_), custom_call_target="tpu_custom_call" | custom-call | tf_op jit(solution)/shard_map/pallas_call | solution.py:128
  60.8 25.9 %shard_map.106 = (bf16[512,256]{1,0:T(8,128)(2,1)}, f32[256,256]{1,0:T(8,128)}, bf16[4,512,256]{2,1,0:T(8,128)(2,1)}) custom-call(bf16[4,512,256]{2,1,0:T(8,128)(2,1)} %bitcast.18, bf16[512,256]{1,0:T(8,128)(2,1)} %cot.1, bf16[256,256]{1,0:T(8,128)(2,1)} %weight.1), custom_call_target="tpu_custom_call" | custom-call | tf_op jit(solution)/shard_map/pallas_call | solution.py:377
  86.7 0.0 copy-start.2
  86.7 10.6 %shard_map.107 = bf16[4,4,4,128,256]{4,3,2,1,0:T(8,128)(2,1)} custom-call(s32[4]{0:T(128)} %bitcast.25, s32[384]{0:T(512)} %reshape.46.refs_1_.row_ref, s32[384]{0:T(512)} %reshape.47.refs_2_.col_ref, bf16[4,96,128,128]{3,2,1,0:T(8,128)(2,1)} %bitcast.15, bf16[16,128,256]{2,1,0:T(8,128)(2,1)} %bitcast.19), custom_call_target="tpu_custom_call" | custom-call | tf_op jit(solution)/shard_map/pallas_call | solution.py:128
  97.3 0.0 copy-start.1
  97.4 0.0 copy-done.2
  97.4 0.7 reshape.55.part
  98.1 1.0 fusion.3.pick
  99.0 49.8 %shard_map.108 = (bf16[512,256]{1,0:T(8,128)(2,1)}, f32[4,8,16,128]{3,2,1,0:T(8,128)}) custom-call(bf16[4,4,512,256]{3,2,1,0:T(8,128)(2,1)} %bitcast.16, bf16[512,512]{1,0:T(8,128)(2,1)} %fusion.3.pick, f32[4,8,16,128]{3,2,1,0:T(8,128)} %reshape.55.part), custom_call_target="tpu_custom_call" | custom-call | tf_op jit(solution)/shard_map/pallas_call | solution.py:341
  148.8 1.7 %reshape.56 = f32[256,256]{1,0:T(8,128)} reshape(f32[4,8,16,128]{3,2,1,0:T(8,128)} %get-tuple-element.12) | data formatting | bytes 524288 | tf_op jit(solution)/shard_map/reshape | solution.py:364
  150.6 0.0 copy-done.1
  150.6 0.7 copy.13
  151.3 1.7 %copy.14 = bf16[512,256]{1,0:T(8,128)(2,1)} copy(bf16[512,256]{1,0:T(8,128)(2,1)} %get-tuple-element.17) | data formatting | bytes 524288
  (2 shorter events, 0.0 us)
Async XLA Ops:
  0.6 1.2 copy-start
  0.6 43.5 %copy-start.3 = (s32[1,1,4,96]{3,2,1,0:T(4,128)S(1)}, s32[1,1,4,96]{3,2,1,0:T(4,128)}, u32[]{:S(2)}) copy-start(s32[1,1,4,96]{3,2,1,0:T(4,128)} %param.10) | copy-start | bytes 4612
  0.7 44.2 %copy-start.4 = (s32[1,1,4,96]{3,2,1,0:T(4,128)S(1)}, s32[1,1,4,96]{3,2,1,0:T(4,128)}, u32[]{:S(2)}) copy-start(s32[1,1,4,96]{3,2,1,0:T(4,128)} %param.11) | copy-start | bytes 4612
  86.7 10.7 %copy-start.2 = (f32[256,256]{1,0:T(8,128)S(1)}, f32[256,256]{1,0:T(8,128)}, u32[]{:S(2)}) copy-start(f32[256,256]{1,0:T(8,128)} %get-tuple-element.10) | copy-start | bytes 786436
  97.3 53.2 %copy-start.1 = (bf16[512,256]{1,0:T(8,128)(2,1)S(1)}, bf16[512,256]{1,0:T(8,128)(2,1)}, u32[]{:S(2)}) copy-start(bf16[512,256]{1,0:T(8,128)(2,1)} %get-tuple-element.16) | copy-start | bytes 786436
where the time goes:
time: 152 us; the launch traced here: 153 us
  Pallas kernels  141 us (93%)
  local copies, waits for them, and re-layouts  6.58 us (4%)
  matrix products  2.91 us (2%)
  other arithmetic  1.74 us (1%)
    pallas_call x1, Pallas kernels, finish_call(): pl.pallas_call(functools.partial(finish_kernel, nodes, reps, scale), out_...  49.8 us
    pallas_call x1, Pallas kernels, halo_call(): pl.pallas_call(functools.partial(halo_kernel, lax.axis_size('node')), out...  41.2 us
    pallas_call x1, Pallas kernels, dense_call(): pl.pallas_call(dense_kernel, out_shape=(jax.ShapeDtypeStruct(half, jnp.bf...  25.9 us
    pallas_call x3, Pallas kernels, tile_call(): pl.pallas_call(kernel, out_shape=jax.ShapeDtypeStruct(out_shape, out_dtyp...  24.1 us

commit v1 on v0

v1 whole, which is shorter than its diff:
```python
import functools
import math

import jax
import jax.numpy as jnp
from jax import lax
from jax.experimental import pallas as pl
from jax.experimental.pallas import tpu as pltpu
from jax.sharding import PartitionSpec as P

EXCL = 3
SHARED = 2
EARLY = 3
GROUP = 14
FIELDS = 4
F32 = jnp.float32
BF16 = jnp.bfloat16


def table_kernel(capacity, count_ref, rows, cols, out, stage):
    lanes = stage.shape[1]
    stage[...] = jnp.zeros_like(stage)
    stage[0:4, 0:capacity] = rows[...].astype(F32)
    stage[4:8, 0:capacity] = cols[...].astype(F32)
    by_slot = stage[...].T
    sub = lax.broadcasted_iota(jnp.int32, (lanes, lanes), 0)
    lane = lax.broadcasted_iota(jnp.int32, (lanes, lanes), 1)
    lane_f = lane.astype(F32)
    before = (lane < sub).astype(BF16)
    upper = (sub < lane).astype(BF16)
    head = lax.broadcasted_iota(jnp.int32, (8, lanes), 0)
    for way in range(2):
        for k in range(4):
            key = by_slot[:, way * 4 + k : way * 4 + k + 1]
            live = sub < count_ref[k]
            mine = jnp.where(live & (key == lane_f), 1.0, 0.0)
            ahead = jnp.dot(before, mine.astype(BF16), preferred_element_type=F32)
            held = jnp.sum(mine, axis=0, keepdims=True)
            pairs = jnp.floor((held + 1.0) * 0.5)
            base = jnp.dot(
                jnp.broadcast_to(pairs, (8, lanes)).astype(BF16), upper, preferred_element_type=F32
            )[0:1]
            rank = jnp.sum(mine * ahead, axis=1, keepdims=True)
            spot = jnp.sum(mine * (2.0 * base), axis=1, keepdims=True) + rank
            put = jnp.where(live & (spot == lane_f), 1.0, 0.0)
            starts = jnp.sum(jnp.where(rank == 0.0, put, 0.0), axis=0, keepdims=True)
            other = stage[(1 - way) * 4 + k : (1 - way) * 4 + k + 1, :]
            values = jnp.where(
                head == 0, lane_f[0:8], jnp.where(head == 1, jnp.broadcast_to(other, (8, lanes)), 1.0)
            )
            found = jnp.dot(values.astype(BF16), put.astype(BF16), preferred_element_type=F32)
            slot = jnp.where(found[2:3] > 0.0, found[0:1], float(capacity))
            last = jnp.where(held > 0.0, base + pairs, 0.0)
            at = (way * 4 + k) * FIELDS
            out[at : at + 1, :] = slot.astype(jnp.int32)
            out[at + 1 : at + 2, :] = found[1:2].astype(jnp.int32)
            out[at + 2 : at + 3, :] = (1.0 - starts).astype(jnp.int32)
            out[at + 3 : at + 4, :] = last.astype(jnp.int32)


def table_call(count, rows, cols):
    capacity = rows.shape[-1]
    vmem = pl.BlockSpec(memory_space=pltpu.VMEM)
    return pl.pallas_call(
        functools.partial(table_kernel, capacity),
        out_shape=jax.ShapeDtypeStruct((8 * FIELDS, 128), jnp.int32),
        in_specs=[pl.BlockSpec(memory_space=pltpu.SMEM), vmem, vmem],
        out_specs=vmem,
        scratch_shapes=[pltpu.VMEM((128, 128), F32)],
        compiler_params=pltpu.CompilerParams(vmem_limit_bytes=4 * 1024 * 1024),
    )(count, rows, cols)


class Wires:
    def __init__(self, send, recv):
        self.send, self.recv, self.used = send, recv, 0

    def copy(self, src, dst, axis, target):
        at = self.used
        self.used += 1
        return pltpu.make_async_remote_copy(
            src_ref=src,
            dst_ref=dst,
            send_sem=self.send.at[at],
            recv_sem=self.recv.at[at],
            device_id={axis: target},
            device_id_type=pl.DeviceIdType.MESH,
        )

    def hop(self, src, dst, axis, target):
        copy = self.copy(src, dst, axis, target)
        copy.start()
        return copy


def fused_kernel(
    nodes, scale, table, tiles, features, order, cot, weight, act, grad, wgrad,
    held, here, halo_a, halo_b, halo_c, sums, acc, part, near, outgoing, far, agg, pg, full,
    terms, tnear, tout, tfar, leaving, got, lleave, lgot, total, lout, lfar,
    wmine, wnear, wout, wfar, wstep, wgot, wfull, pick,
    load_sems, send, recv,
):
    capacity = tiles.shape[1]
    count, size, feat = here.shape
    tq = count // 4
    quarter = tq * size
    pairs = (capacity + count) // 2
    me, home = lax.axis_index("rep"), lax.axis_index("node")
    x, c = me // 2, me % 2
    sib, across, diag = x * 2 + 1 - c, (1 - x) * 2 + c, (1 - x) * 2 + 1 - c
    wires = Wires(send, recv)

    def to_node(d):
        return (home + d) % nodes

    doubling = [1 << i for i in range(nodes.bit_length() - 1)]
    partners = []
    for step in doubling:
        low = (home // step) % 2
        partners.append(home + step - 2 * step * low)
    peers = [("rep", sib), ("rep", across)]
    peers += [("node", to_node(d)) for d in (1, nodes - 1, 2, nodes - 2)]
    peers += [("node", p) for p in partners]
    barrier = pltpu.get_barrier_semaphore()
    for axis, target in peers:
        pl.semaphore_signal(
            barrier, inc=1, device_id={axis: target}, device_id_type=pl.DeviceIdType.MESH
        )

    loads = [
        pltpu.make_async_copy(
            tiles.at[k], held.at[k, pl.ds(0, capacity)], load_sems.at[k]
        )
        for k in (1, 0, 2, 3)
    ]
    for load in loads:
        load.start()

    spots = lax.broadcasted_iota(jnp.int32, (quarter, size), 0)

    def chosen(t):
        return (spots == lax.rem(order[pl.ds(t, 1), :], quarter)).astype(BF16)

    def reorder(t):
        rows = features[pl.ds(pl.multiple_of((t // tq) * quarter, quarter), quarter), :]
        here[t] = lax.dot_general(
            chosen(t), rows, (((0,), (0,)), ((), ())), preferred_element_type=F32
        ).astype(BF16)

    first = 10 * x + EXCL * c
    common = 2 * 2 * EXCL // 2 + SHARED * c
    other = 10 * (1 - x) + EXCL * c
    for i in range(EXCL):
        reorder(first + i)
    for i in range(SHARED):
        reorder(common + i)
    pl.semaphore_wait(barrier, len(peers))

    moves = ((nodes - 1, halo_a), (1, halo_b), (2, halo_c))
    direct, shared = [], []
    for d, land in moves:
        direct.append(
            [
                wires.hop(here.at[first + i], land.at[first + i], "node", to_node(d))
                for i in range(EXCL)
            ]
        )
        block = pl.ds(common, SHARED)
        shared.append(wires.hop(here.at[block], land.at[block], "node", to_node(d)))
    for i in range(EXCL):
        reorder(other + i)
    rest = 10 * x + EXCL * (1 - c)
    for i in range(EXCL):
        reorder(rest + i)
        reorder(10 * (1 - x) + EXCL * (1 - c) + i)
    for i in range(SHARED):
        reorder(2 * EXCL + SHARED * (1 - c) + i)
    for k in range(4):
        held[k, capacity] = jnp.zeros((size, size), BF16)
    sums[0] = jnp.zeros((size, feat), F32)
    mine_pick = jnp.concatenate([chosen(me * tq + i) for i in range(tq)], axis=1)
    pick[...] = mine_pick

    crossing, aside_direct, aside_cross, aside_shared = [], [], [], []
    for d, land in moves:
        for i in range(EXCL):
            near_tile, far_tile = land.at[first + i], land.at[other + i]
            crossing.append(wires.copy(near_tile, near_tile, "rep", across))
            aside_direct.append(wires.copy(near_tile, near_tile, "rep", sib))
            aside_cross.append(wires.copy(far_tile, far_tile, "rep", sib))
        both = land.at[pl.ds(common, SHARED)]
        aside_shared.append(wires.copy(both, both, "rep", sib))

    def event_direct(g):
        direct[g // EXCL][g % EXCL].wait()
        crossing[g].start()
        aside_direct[g].start()

    def event_cross(g):
        crossing[g].wait()
        aside_cross[g].start()

    def event_shared(j):
        shared[j].wait()
        aside_shared[j].start()

    def settle(j):
        for i in range(EXCL):
            aside_direct[j * EXCL + i].wait()
            aside_cross[j * EXCL + i].wait()
        aside_shared[j].wait()

    def product(way, k, i, source):
        at = (way * 4 + k) * FIELDS
        one, two = held[k, table[at, 2 * i]], held[k, table[at, 2 * i + 1]]
        left, right = source[table[at + 1, 2 * i]], source[table[at + 1, 2 * i + 1]]
        rows = jnp.concatenate([left, right], axis=0)
        if way == 0:
            return jnp.dot(
                jnp.concatenate([one, two], axis=1), rows, preferred_element_type=F32
            )
        return lax.dot_general(
            jnp.concatenate([one, two], axis=0), rows, (((0,), (0,)), ((), ())),
            preferred_element_type=F32,
        )

    def sweep(way, k, source, events):
        at = (way * 4 + k) * FIELDS

        def body(step, _):
            for turn, work in enumerate(events):
                if work:
                    @pl.when(step == turn)
                    def _(work=work):
                        for f in work:
                            f()
            base = step * GROUP
            products = [product(way, k, base + g, source) for g in range(GROUP)]
            value = sums[base]
            for g in range(GROUP):
                value = products[g] + table[at + 2, 2 * (base + g)].astype(F32) * value
                sums[base + g + 1] = value
            return 0

        lax.fori_loop(0, pairs // GROUP, body, 0)

    def ends(way, k, r):
        return sums[table[(way * 4 + k) * FIELDS + 3, r]]

    def run(*work):
        for f in work:
            f()

    E = lambda g: (lambda: event_direct(g))
    X = lambda g: (lambda: event_cross(g))
    S = lambda j: (lambda: event_shared(j))

    for load in loads:
        load.wait()
    sweep(0, 1, here, [[E(0)], [E(1)], [E(2), X(0)], [E(3), X(1)]])
    for r in range(count):
        acc[r] = ends(0, 1, r)
    run(E(4), X(2), S(0))
    settle(0)
    sweep(0, 0, halo_a, [[E(5), X(3)], [E(6), X(4)], [E(7), X(5)], [E(8), X(6)]])
    for r in range(count):
        acc[r] += ends(0, 0, r)
    run(S(1))
    settle(1)
    sweep(0, 2, halo_b, [[X(7)], [X(8), S(2)], [], []])
    for r in range(count):
        acc[r] += ends(0, 2, r)
    settle(2)
    sweep(0, 3, halo_c, [[], [], [], []])

    def finish_rows(q):
        for i in range(tq):
            r = q * tq + i
            value = acc[r] + ends(0, 3, r)
            acc[r] = value
            part[r] = value.astype(BF16)

    finish_rows(diag)
    to_sib = [
        wires.hop(part.at[diag * tq + i], near.at[i], "rep", sib) for i in range(tq)
    ]
    finish_rows(sib)
    block = pl.ds(sib * tq, tq)
    rest_sib = wires.hop(part.at[block], near.at[pl.ds(tq, tq)], "rep", sib)
    finish_rows(across)
    crossed = []
    for i in range(tq):
        to_sib[i].wait()
        outgoing[i] = (acc[across * tq + i] + near[i].astype(F32)).astype(BF16)
        crossed.append(wires.hop(outgoing.at[i], far.at[i], "rep", across))
    finish_rows(me)
    rest_sib.wait()
    over, side, relay = [], [], []
    for i in range(tq):
        r = me * tq + i
        mine = acc[r] + near[tq + i].astype(F32)
        crossed[i].wait()
        aggregate = (mine + far[i].astype(F32)).astype(BF16)
        agg[i * size : (i + 1) * size, :] = aggregate
        pre_act = jnp.dot(aggregate, weight[...], preferred_element_type=F32)
        gate = jax.nn.sigmoid(pre_act)
        act[i * size : (i + 1) * size, :] = (pre_act * gate).astype(act.dtype)
        pre_grad = (
            cot[i * size : (i + 1) * size, :].astype(F32) * gate * (1.0 + pre_act * (1.0 - gate))
        ).astype(BF16)
        pg[i * size : (i + 1) * size, :] = pre_grad
        full[r] = lax.dot_general(
            pre_grad, weight[...], (((1,), (1,)), ((), ())), preferred_element_type=F32
        ).astype(BF16)
        over.append(wires.hop(full.at[r], full.at[r], "rep", across))
        side.append(wires.hop(full.at[r], full.at[r], "rep", sib))
    wrows = feat // 4
    wpart = lax.dot_general(
        agg[...], pg[...], (((0,), (0,)), ((), ())), preferred_element_type=F32
    )
    for q in range(4):
        wmine[q] = wpart[q * wrows : (q + 1) * wrows, :].astype(BF16)
    for i in range(tq):
        over[i].wait()
        r = across * tq + i
        relay.append(wires.hop(full.at[r], full.at[r], "rep", sib))
    wsib = [
        wires.hop(wmine.at[diag], wnear.at[0], "rep", sib),
        wires.hop(wmine.at[sib], wnear.at[1], "rep", sib),
    ]
    for copy in side + relay:
        copy.wait()

    late = tq - EARLY
    flight = {}
    for k, j, d in ((0, 0, 1), (2, 1, nodes - 1), (3, 2, nodes - 2), (1, 3, 0)):
        flight[k, "diag"] = wires.copy(
            terms.at[k, pl.ds(diag * tq, tq)], tnear.at[k, pl.ds(0, tq)], "rep", sib
        )
        flight[k, "sib"] = wires.copy(
            terms.at[k, pl.ds(sib * tq, tq)], tnear.at[k, pl.ds(tq, tq)], "rep", sib
        )
        flight[k, "x"] = wires.copy(tout.at[k], tfar.at[k], "rep", across)
        if d:
            flight[k, "late"] = wires.copy(lleave.at[j], lgot.at[j], "node", to_node(d))
            flight[k, "node"] = wires.copy(leaving.at[j], got.at[j], "node", to_node(d))
    wflight = {
        "x": wires.copy(wout, wfar, "rep", across),
        "over": wires.copy(wfull.at[me], wfull.at[me], "rep", across),
        "side": wires.copy(wfull.at[me], wfull.at[me], "rep", sib),
        "relay": wires.copy(wfull.at[across], wfull.at[across], "rep", sib),
    }
    for i, partner in enumerate(partners):
        wflight[i] = wires.copy(wstep.at[i], wgot.at[i], "node", partner)

    def terms_out(k):
        for r in range(count):
            terms[k, r] = ends(1, k, r).astype(BF16)
        flight[k, "diag"].start()
        flight[k, "sib"].start()

    def terms_cross(k, j, d):
        flight[k, "diag"].wait()
        for i in range(tq):
            value = terms[k, across * tq + i].astype(F32) + tnear[k, i].astype(F32)
            if i < EARLY:
                tout[k, i] = value.astype(BF16)
            elif d:
                lleave[j, i - EARLY] = value.astype(BF16)
            else:
                total[tq + i - EARLY] = value
        flight[k, "x"].start()
        if d:
            flight[k, "late"].start()

    def terms_leave(k, j, d):
        flight[k, "sib"].wait()
        flight[k, "x"].wait()
        for i in range(tq):
            value = terms[k, me * tq + i].astype(F32) + tnear[k, tq + i].astype(F32)
            if i < EARLY:
                value = value + tfar[k, i].astype(F32)
            if d:
                leaving[j, i] = value.astype(BF16)
            else:
                total[i] = value
        if d:
            flight[k, "node"].start()

    def wgrad_cross():
        for copy in wsib:
            copy.wait()
        wout[...] = (wmine[across].astype(F32) + wnear[0].astype(F32)).astype(BF16)
        wflight["x"].start()

    def wgrad_double(i):
        if i == 0:
            wflight["x"].wait()
            value = wmine[me].astype(F32) + wnear[1].astype(F32) + wfar[...].astype(F32)
        else:
            wflight[i - 1].wait()
            value = wstep[i - 1].astype(F32) + wgot[i - 1].astype(F32)
        if i < len(doubling):
            wstep[i] = value.astype(BF16)
            wflight[i].start()
        else:
            wfull[me] = (value * scale).astype(BF16)
            wflight["over"].start()
            wflight["side"].start()

    def wgrad_relay():
        wflight["over"].wait()
        wflight["relay"].start()

    C = lambda k, j, d: (lambda: terms_cross(k, j, d))
    L = lambda k, j, d: (lambda: terms_leave(k, j, d))
    W = lambda i: (lambda: wgrad_double(i))
    leg = {0: (0, 0, 1), 2: (2, 1, nodes - 1), 3: (3, 2, nodes - 2), 1: (1, 3, 0)}
    sweep(1, 0, full, [[], [], [wgrad_cross], []])
    terms_out(0)
    sweep(1, 2, full, [[], [C(*leg[0])], [W(0)], []])
    terms_out(2)
    sweep(1, 3, full, [[], [C(*leg[2])], [W(1)], []])
    terms_out(3)
    sweep(1, 1, full, [[L(*leg[0])], [C(*leg[3])], [W(2)], []])
    terms_out(1)
    terms_leave(*leg[2])
    terms_cross(*leg[1])
    for i in range(3, len(doubling) + 1):
        wgrad_double(i)
    terms_leave(*leg[3])
    spare = [total[tq + i] for i in range(late)]
    for j, k in enumerate((0, 2, 3)):
        flight[k, "late"].wait()
        spare = [spare[i] + lgot[j, i].astype(F32) for i in range(late)]
    for i in range(late):
        lout[i] = spare[i].astype(BF16)
    last_cross = wires.hop(lout, lfar, "rep", across)
    wgrad_relay()
    terms_leave(*leg[1])
    wflight["side"].wait()
    wflight["relay"].wait()
    for q in range(4):
        wgrad[q * wrows : (q + 1) * wrows, :] = wfull[q].astype(F32)
    for k in (0, 2, 3):
        flight[k, "node"].wait()
    last_cross.wait()
    values = []
    for i in range(tq):
        value = total[i]
        for j in range(3):
            value = value + got[j, i].astype(F32)
        if i >= EARLY:
            value = value + lfar[i - EARLY].astype(F32)
        values.append(value.astype(BF16))
    grad[...] = jnp.dot(
        pick[...], jnp.concatenate(values, axis=0), preferred_element_type=F32
    ).astype(grad.dtype)


def fused_call(nodes, scale, table, tiles, features, order, cot, weight):
    capacity, size = tiles.shape[1], tiles.shape[-1]
    feat = features.shape[1]
    count = features.shape[0] // size
    tq = count // 4
    late = tq - EARLY
    pairs = (capacity + count) // 2
    steps = nodes.bit_length() - 1
    vmem = pl.BlockSpec(memory_space=pltpu.VMEM)

    def rows(*lead):
        return pltpu.VMEM(lead + (size, feat), BF16)

    def sums(*lead):
        return pltpu.VMEM(lead + (size, feat), F32)

    def wide(*lead):
        return pltpu.VMEM(lead + (feat // 4, feat), BF16)

    flat = pltpu.VMEM((tq * size, feat), BF16)
    return pl.pallas_call(
        functools.partial(fused_kernel, nodes, scale),
        out_shape=(
            jax.ShapeDtypeStruct(cot.shape, BF16),
            jax.ShapeDtypeStruct(cot.shape, BF16),
            jax.ShapeDtypeStruct((feat, feat), F32),
        ),
        in_specs=[pl.BlockSpec(memory_space=pltpu.SMEM), pl.BlockSpec(memory_space=pl.ANY)]
        + [vmem] * 4,
        out_specs=(vmem,) * 3,
        scratch_shapes=[
            pltpu.VMEM((4, capacity + 1, size, size), BF16),
            rows(count), rows(count), rows(count), rows(count),
            sums(pairs + 1), sums(count),
            rows(count), rows(2 * tq), rows(tq), rows(tq), flat, flat, rows(count),
            rows(4, count), rows(4, 2 * tq), rows(4, EARLY), rows(4, EARLY),
            rows(3, tq), rows(3, tq), rows(3, late), rows(3, late),
            sums(tq + late), rows(late), rows(late),
            wide(4), wide(2), wide(), wide(), wide(steps), wide(steps), wide(4),
            pltpu.VMEM((tq * size, tq * size), BF16),
            pltpu.SemaphoreType.DMA((4,)),
            pltpu.SemaphoreType.DMA((128,)),
            pltpu.SemaphoreType.DMA((128,)),
        ],
        compiler_params=pltpu.CompilerParams(
            collective_id=0, has_side_effects=True, vmem_limit_bytes=60 * 1024 * 1024
        ),
    )(table, tiles, features, order, cot, weight)


def local(features, tiles, tile_rows, tile_cols, tile_count, order, weight, cotangent):
    nodes = lax.axis_size("node")
    size = tiles.shape[-1]
    scale = 1.0 / math.sqrt(features.shape[0] * nodes)
    table = table_call(tile_count.reshape(-1), tile_rows[0, 0], tile_cols[0, 0])
    activated, feature_grad, weight_grad = fused_call(
        nodes, scale, table, tiles[0, 0], features, order.reshape(-1, size), cotangent, weight
    )
    return (activated, feature_grad, weight_grad)


def solution(mesh):
    placed = (
        P("node", None),
        P("node", "rep", None, None, None, None),
        P("node", "rep", None, None),
        P("node", "rep", None, None),
        P("node", "rep", None),
        P("node"),
        P(),
        P(("node", "rep"), None),
    )
    return jax.shard_map(
        local,
        mesh=mesh,
        in_specs=placed,
        out_specs=(P(("node", "rep"), None), P(("node", "rep"), None), P()),
        check_vma=False,
    )
```

time: 152 us -> 93.5 us (0.62)
  Pallas kernels: 141 us -> 84.9 us
  matrix products: 2.91 us -> 0 us
  other arithmetic: 1.74 us -> 0 us
    pallas_call x6 -> x2, Pallas kernels: 141 us -> 84.9 us  [the longest x1 82.2 us: fused_call(): pl.pallas_call(functools.partial(fused_kernel, nodes, scale), out_shape=(...]
    unnamed x12 -> x11, local copies, waits for them, and re-layouts: 2.79 us -> 7.63 us
    reshape x5 -> x0, local copies, waits for them, and re-layouts: 3.78 us -> none  [the longest x1 1.73 us: finish_call(): return (grad, out.reshape(part.shape))]
    dot_general x2 -> x0, matrix products: 2.91 us -> none  [the longest x1 1.85 us: local(): jnp.einsum('qpi,qif->qpf', pick, features.reshape(reps, quarter, feat), p...]
where the time goes in v1:
time: 93.5 us; the launch traced here: 93.2 us
  Pallas kernels  84.9 us (91%)
  local copies, waits for them, and re-layouts  7.63 us (8%)
    pallas_call x1, Pallas kernels, fused_call(): pl.pallas_call(functools.partial(fused_kernel, nodes, scale), out_shape=(...  82.2 us
    unnamed x11, local copies, waits for them, and re-layouts  7.63 us
    pallas_call x1, Pallas kernels, table_call(): pl.pallas_call(functools.partial(table_kernel, capacity), out_shape=jax.S...  2.74 us

profile of v1, /device:TPU:0, one launch (start us, length us, event | category | flops | bytes accessed | tf_op | source)
XLA Modules:
  0.0 93.2 jit_solution(4637896479945734510)
XLA Ops:
  0.6 0.0 copy-start.1
  0.6 0.7 copy-done.1
  1.3 0.0 copy-start.2
  1.3 0.7 copy-done.2
  2.0 0.0 copy-start.3
  2.0 0.7 copy-done.3
  2.7 2.7 %shard_map.103.table = s32[32,128]{1,0:T(8,128)S(1)} custom-call(s32[4]{0:T(128)S(1)} %bitcast.7, s32[4,96]{1,0:T(4,128)S(1)} %bitcast.5, s32[4,96]{1,0:T(4,128)S(1)} %bitcast.6), custom_call_target="tpu_custom_call" | custom-call | tf_op jit(solution)/shard_map/pallas_call | solution.py:64
  5.4 0.0 copy-start
  5.4 0.6 copy-done
  6.0 82.2 %shard_map.104 = (bf16[512,256]{1,0:T(8,128)(2,1)}, bf16[512,256]{1,0:T(8,128)(2,1)}, f32[256,256]{1,0:T(8,128)}) custom-call(s32[32,128]{1,0:T(8,128)} %copy-done, bf16[4,96,128,128]{3,2,1,0:T(8,128)(2,1)} %bitcast.8, bf16[2048,256]{1,0:T(8,128)(2,1)} %features.1, s32[16,128]{1,0:T(8,128)} %bitcast.9, bf16[512,256]{1,0:T(8,128)(2,1)} %cot.1, ...), custom_call_target="tpu_custom_call" | custom-call | tf_op jit(solution)/shard_map/pallas_call | solution.py:481
  88.2 1.7 %copy.14 = bf16[512,256]{1,0:T(8,128)(2,1)} copy(bf16[512,256]{1,0:T(8,128)(2,1)} %get-tuple-element.6) | data formatting | bytes 524288
  89.9 1.7 %copy.15 = bf16[512,256]{1,0:T(8,128)(2,1)} copy(bf16[512,256]{1,0:T(8,128)(2,1)} %get-tuple-element.7) | data formatting | bytes 524288
  91.6 1.7 %copy.16 = f32[256,256]{1,0:T(8,128)} copy(f32[256,256]{1,0:T(8,128)} %get-tuple-element.8) | data formatting | bytes 524288
Async XLA Ops:
  0.6 0.7 copy-start.1
  1.3 0.7 copy-start.2
  2.0 0.7 copy-start.3
  5.4 0.6 copy-start

commit v2 on v1

--- a/solution.py
+++ b/solution.py
@@ -12,12 +12,21 @@
 SHARED = 2
 EARLY = 3
 GROUP = 14
+VLIM = 60
 FIELDS = 4
 F32 = jnp.float32
 BF16 = jnp.bfloat16
 
 
-def table_kernel(capacity, count_ref, rows, cols, out, stage):
+def table_kernel(capacity, count_src, row_src, col_src, out, stage, count_ref, rows, cols, sems):
+    copies = [
+        pltpu.make_async_copy(src, dst, sems.at[i])
+        for i, (src, dst) in enumerate(((count_src, count_ref), (row_src, rows), (col_src, cols)))
+    ]
+    for copy in copies:
+        copy.start()
+    for copy in copies:
+        copy.wait()
     lanes = stage.shape[1]
     stage[...] = jnp.zeros_like(stage)
     stage[0:4, 0:capacity] = rows[...].astype(F32)
@@ -32,7 +41,7 @@
     for way in range(2):
         for k in range(4):
             key = by_slot[:, way * 4 + k : way * 4 + k + 1]
-            live = sub < count_ref[k]
+            live = sub < count_ref[0, k]
             mine = jnp.where(live & (key == lane_f), 1.0, 0.0)
             ahead = jnp.dot(before, mine.astype(BF16), preferred_element_type=F32)
             held = jnp.sum(mine, axis=0, keepdims=True)
@@ -58,17 +67,22 @@
             out[at + 3 : at + 4, :] = last.astype(jnp.int32)
 
 
-def table_call(count, rows, cols):
-    capacity = rows.shape[-1]
-    vmem = pl.BlockSpec(memory_space=pltpu.VMEM)
+def table_call(counts, row_ids, col_ids):
+    capacity = row_ids.shape[-1]
     return pl.pallas_call(
         functools.partial(table_kernel, capacity),
         out_shape=jax.ShapeDtypeStruct((8 * FIELDS, 128), jnp.int32),
-        in_specs=[pl.BlockSpec(memory_space=pltpu.SMEM), vmem, vmem],
-        out_specs=vmem,
-        scratch_shapes=[pltpu.VMEM((128, 128), F32)],
-        compiler_params=pltpu.CompilerParams(vmem_limit_bytes=4 * 1024 * 1024),
-    )(count, rows, cols)
+        in_specs=[pl.BlockSpec(memory_space=pl.ANY)] * 3,
+        out_specs=pl.BlockSpec(memory_space=pltpu.VMEM),
+        scratch_shapes=[
+            pltpu.VMEM((128, 128), F32),
+            pltpu.SMEM(counts.shape, jnp.int32),
+            pltpu.VMEM(row_ids.shape, jnp.int32),
+            pltpu.VMEM(col_ids.shape, jnp.int32),
+            pltpu.SemaphoreType.DMA((3,)),
+        ],
+        compiler_params=pltpu.CompilerParams(vmem_limit_bytes=VLIM * 1024 * 1024),
+    )(counts, row_ids, col_ids)
 
 
 class Wires:
@@ -94,11 +108,12 @@
 
 
 def fused_kernel(
-    nodes, scale, table, tiles, features, order, cot, weight, act, grad, wgrad,
+    nodes, scale, table, tiles, feature_src, order_src, cot_src, weight_src,
+    act, grad, wgrad, features, order, cot, weight,
     held, here, halo_a, halo_b, halo_c, sums, acc, part, near, outgoing, far, agg, pg, full,
     terms, tnear, tout, tfar, leaving, got, lleave, lgot, total, lout, lfar,
     wmine, wnear, wout, wfar, wstep, wgot, wfull, pick,
-    load_sems, send, recv,
+    load_sems, stage_sems, send, recv,
 ):
     capacity = tiles.shape[1]
     count, size, feat = here.shape
@@ -127,6 +142,16 @@
             barrier, inc=1, device_id={axis: target}, device_id_type=pl.DeviceIdType.MESH
         )
 
+    staged = [
+        pltpu.make_async_copy(src, dst, stage_sems.at[i])
+        for i, (src, dst) in enumerate(
+            (
+                (order_src, order), (feature_src, features), (cot_src, cot), (weight_src, weight),
+            )
+        )
+    ]
+    for copy in staged:
+        copy.start()
     loads = [
         pltpu.make_async_copy(
             tiles.at[k], held.at[k, pl.ds(0, capacity)], load_sems.at[k]
@@ -150,13 +175,15 @@
     first = 10 * x + EXCL * c
     common = 2 * 2 * EXCL // 2 + SHARED * c
     other = 10 * (1 - x) + EXCL * c
+    for copy in staged[:2]:
+        copy.wait()
     for i in range(EXCL):
         reorder(first + i)
     for i in range(SHARED):
         reorder(common + i)
     pl.semaphore_wait(barrier, len(peers))
 
-    moves = ((nodes - 1, halo_a), (1, halo_b), (2, halo_c))
+    moves = ((2, halo_a), (nodes - 1, halo_b), (1, halo_c))
     direct, shared = [], []
     for d, land in moves:
         direct.append(
@@ -175,6 +202,8 @@
         reorder(10 * (1 - x) + EXCL * (1 - c) + i)
     for i in range(SHARED):
         reorder(2 * EXCL + SHARED * (1 - c) + i)
+    for copy in staged[2:]:
+        copy.wait()
     for k in range(4):
         held[k, capacity] = jnp.zeros((size, size), BF16)
     sums[0] = jnp.zeros((size, feat), F32)
@@ -262,21 +291,21 @@
         acc[r] = ends(0, 1, r)
     run(E(4), X(2), S(0))
     settle(0)
-    sweep(0, 0, halo_a, [[E(5), X(3)], [E(6), X(4)], [E(7), X(5)], [E(8), X(6)]])
+    sweep(0, 3, halo_a, [[E(5), X(3)], [E(6), X(4)], [E(7), X(5)], [E(8), X(6)]])
+    for r in range(count):
+        acc[r] += ends(0, 3, r)
+    run(S(1))
+    settle(1)
+    sweep(0, 0, halo_b, [[X(7)], [X(8), S(2)], [], []])
     for r in range(count):
         acc[r] += ends(0, 0, r)
-    run(S(1))
-    settle(1)
-    sweep(0, 2, halo_b, [[X(7)], [X(8), S(2)], [], []])
-    for r in range(count):
-        acc[r] += ends(0, 2, r)
     settle(2)
-    sweep(0, 3, halo_c, [[], [], [], []])
+    sweep(0, 2, halo_c, [[], [], [], []])
 
     def finish_rows(q):
         for i in range(tq):
             r = q * tq + i
-            value = acc[r] + ends(0, 3, r)
+            value = acc[r] + ends(0, 2, r)
             acc[r] = value
             part[r] = value.astype(BF16)
 
@@ -340,10 +369,18 @@
         flight[k, "sib"] = wires.copy(
             terms.at[k, pl.ds(sib * tq, tq)], tnear.at[k, pl.ds(tq, tq)], "rep", sib
         )
-        flight[k, "x"] = wires.copy(tout.at[k], tfar.at[k], "rep", across)
+        for i in range(EARLY):
+            flight[k, "x", i] = wires.copy(tout.at[k, i], tfar.at[k, i], "rep", across)
         if d:
             flight[k, "late"] = wires.copy(lleave.at[j], lgot.at[j], "node", to_node(d))
-            flight[k, "node"] = wires.copy(leaving.at[j], got.at[j], "node", to_node(d))
+            for i in range(EARLY):
+                flight[k, "node", i] = wires.copy(
+                    leaving.at[j, i], got.at[j, i], "node", to_node(d)
+                )
+            tail = pl.ds(EARLY, late)
+            flight[k, "node", EARLY] = wires.copy(
+                leaving.at[j, tail], got.at[j, tail], "node", to_node(d)
+            )
     wflight = {
         "x": wires.copy(wout, wfar, "rep", across),
         "over": wires.copy(wfull.at[me], wfull.at[me], "rep", across),
@@ -354,10 +391,12 @@
         wflight[i] = wires.copy(wstep.at[i], wgot.at[i], "node", partner)
 
     def terms_out(k):
-        for r in range(count):
-            terms[k, r] = ends(1, k, r).astype(BF16)
-        flight[k, "diag"].start()
-        flight[k, "sib"].start()
+        for q, name in ((diag, "diag"), (sib, "sib"), (across, None), (me, None)):
+            for i in range(tq):
+                r = q * tq + i
+                terms[k, r] = ends(1, k, r).astype(BF16)
+            if name:
+                flight[k, name].start()
 
     def terms_cross(k, j, d):
         flight[k, "diag"].wait()
@@ -365,27 +404,32 @@
             value = terms[k, across * tq + i].astype(F32) + tnear[k, i].astype(F32)
             if i < EARLY:
                 tout[k, i] = value.astype(BF16)
+                flight[k, "x", i].start()
             elif d:
                 lleave[j, i - EARLY] = value.astype(BF16)
             else:
                 total[tq + i - EARLY] = value
-        flight[k, "x"].start()
         if d:
             flight[k, "late"].start()
-
-    def terms_leave(k, j, d):
         flight[k, "sib"].wait()
-        flight[k, "x"].wait()
-        for i in range(tq):
+        for i in range(EARLY, tq):
             value = terms[k, me * tq + i].astype(F32) + tnear[k, tq + i].astype(F32)
-            if i < EARLY:
-                value = value + tfar[k, i].astype(F32)
             if d:
                 leaving[j, i] = value.astype(BF16)
             else:
                 total[i] = value
         if d:
-            flight[k, "node"].start()
+            flight[k, "node", EARLY].start()
+
+    def terms_leave(k, j, d, i):
+        flight[k, "x", i].wait()
+        value = terms[k, me * tq + i].astype(F32) + tnear[k, tq + i].astype(F32)
+        value = value + tfar[k, i].astype(F32)
+        if d:
+            leaving[j, i] = value.astype(BF16)
+            flight[k, "node", i].start()
+        else:
+            total[i] = value
 
     def wgrad_cross():
         for copy in wsib:
@@ -413,22 +457,25 @@
         wflight["relay"].start()
 
     C = lambda k, j, d: (lambda: terms_cross(k, j, d))
-    L = lambda k, j, d: (lambda: terms_leave(k, j, d))
+    L = lambda k, j, d, i: (lambda: terms_leave(k, j, d, i))
     W = lambda i: (lambda: wgrad_double(i))
     leg = {0: (0, 0, 1), 2: (2, 1, nodes - 1), 3: (3, 2, nodes - 2), 1: (1, 3, 0)}
-    sweep(1, 0, full, [[], [], [wgrad_cross], []])
+    sweep(1, 3, full, [[], [], [wgrad_cross], []])
+    terms_out(3)
+    sweep(1, 0, full, [[], [C(*leg[3])], [W(0)], []])
     terms_out(0)
-    sweep(1, 2, full, [[], [C(*leg[0])], [W(0)], []])
+    sweep(1, 2, full, [[], [C(*leg[0])], [W(1)], []])
     terms_out(2)
-    sweep(1, 3, full, [[], [C(*leg[2])], [W(1)], []])
-    terms_out(3)
-    sweep(1, 1, full, [[L(*leg[0])], [C(*leg[3])], [W(2)], []])
+    sweep(1, 1, full, [[L(*leg[3], 0)], [C(*leg[2]), L(*leg[3], 1)], [W(2), L(*leg[3], 2)], []])
     terms_out(1)
-    terms_leave(*leg[2])
+    terms_leave(*leg[0], 0)
     terms_cross(*leg[1])
+    for i in range(1, EARLY):
+        terms_leave(*leg[0], i)
     for i in range(3, len(doubling) + 1):
         wgrad_double(i)
-    terms_leave(*leg[3])
+    for i in range(EARLY):
+        terms_leave(*leg[2], i)
     spare = [total[tq + i] for i in range(late)]
     for j, k in enumerate((0, 2, 3)):
         flight[k, "late"].wait()
@@ -437,13 +484,15 @@
         lout[i] = spare[i].astype(BF16)
     last_cross = wires.hop(lout, lfar, "rep", across)
     wgrad_relay()
-    terms_leave(*leg[1])
+    for i in range(EARLY):
+        terms_leave(*leg[1], i)
     wflight["side"].wait()
     wflight["relay"].wait()
     for q in range(4):
         wgrad[q * wrows : (q + 1) * wrows, :] = wfull[q].astype(F32)
     for k in (0, 2, 3):
-        flight[k, "node"].wait()
+        for i in range(EARLY + 1):
+            flight[k, "node", i].wait()
     last_cross.wait()
     values = []
     for i in range(tq):
@@ -485,10 +534,13 @@
             jax.ShapeDtypeStruct(cot.shape, BF16),
             jax.ShapeDtypeStruct((feat, feat), F32),
         ),
-        in_specs=[pl.BlockSpec(memory_space=pltpu.SMEM), pl.BlockSpec(memory_space=pl.ANY)]
-        + [vmem] * 4,
+        in_specs=[pl.BlockSpec(memory_space=pltpu.SMEM)] + [pl.BlockSpec(memory_space=pl.ANY)] * 5,
         out_specs=(vmem,) * 3,
         scratch_shapes=[
+            pltpu.VMEM(features.shape, BF16),
+            pltpu.VMEM(order.shape, jnp.int32),
+            pltpu.VMEM(cot.shape, BF16),
+            pltpu.VMEM(weight.shape, BF16),
             pltpu.VMEM((4, capacity + 1, size, size), BF16),
             rows(count), rows(count), rows(count), rows(count),
             sums(pairs + 1), sums(count),
@@ -499,24 +551,53 @@
             wide(4), wide(2), wide(), wide(), wide(steps), wide(steps), wide(4),
             pltpu.VMEM((tq * size, tq * size), BF16),
             pltpu.SemaphoreType.DMA((4,)),
+            pltpu.SemaphoreType.DMA((4,)),
             pltpu.SemaphoreType.DMA((128,)),
             pltpu.SemaphoreType.DMA((128,)),
         ],
         compiler_params=pltpu.CompilerParams(
-            collective_id=0, has_side_effects=True, vmem_limit_bytes=60 * 1024 * 1024
+            collective_id=0, has_side_effects=True, vmem_limit_bytes=VLIM * 1024 * 1024
         ),
     )(table, tiles, features, order, cot, weight)
+
+
+def publish_kernel(*refs):
+    n = (len(refs) - 2) // 3
+    ins, outs, held = refs[:n], refs[n : 2 * n], refs[2 * n : 3 * n]
+    take, give = refs[3 * n], refs[3 * n + 1]
+    loads = [pltpu.make_async_copy(ins[i], held[i], take.at[i]) for i in range(n)]
+    stores = [pltpu.make_async_copy(held[i], outs[i], give.at[i]) for i in range(n)]
+    for load in loads:
+        load.start()
+    for load, store in zip(loads, stores):
+        load.wait()
+        store.start()
+    for store in stores:
+        store.wait()
+
+
+def publish_call(*arrays):
+    n = len(arrays)
+    return pl.pallas_call(
+        publish_kernel,
+        out_shape=tuple(jax.ShapeDtypeStruct(a.shape, a.dtype) for a in arrays),
+        in_specs=[pl.BlockSpec(memory_space=pl.ANY)] * n,
+        out_specs=(pl.BlockSpec(memory_space=pl.ANY),) * n,
+        scratch_shapes=[pltpu.VMEM(a.shape, a.dtype) for a in arrays]
+        + [pltpu.SemaphoreType.DMA((n,))] * 2,
+        compiler_params=pltpu.CompilerParams(vmem_limit_bytes=VLIM * 1024 * 1024),
+    )(*arrays)
 
 
 def local(features, tiles, tile_rows, tile_cols, tile_count, order, weight, cotangent):
     nodes = lax.axis_size("node")
     size = tiles.shape[-1]
     scale = 1.0 / math.sqrt(features.shape[0] * nodes)
-    table = table_call(tile_count.reshape(-1), tile_rows[0, 0], tile_cols[0, 0])
-    activated, feature_grad, weight_grad = fused_call(
+    table = table_call(tile_count[0], tile_rows[0, 0], tile_cols[0, 0])
+    outs = fused_call(
         nodes, scale, table, tiles[0, 0], features, order.reshape(-1, size), cotangent, weight
     )
-    return (activated, feature_grad, weight_grad)
+    return publish_call(*outs)
 
 
 def solution(mesh):

time: 93.5 us -> 84.9 us (0.908)
  local copies, waits for them, and re-layouts: 7.63 us -> 0 us
  Pallas kernels: 84.9 us -> 83.9 us
    unnamed x11 -> x0, local copies, waits for them, and re-layouts: 7.63 us -> none
    pallas_call x1, Pallas kernels: 82.2 us -> 78.4 us  [fused_call(): pl.pallas_call(functools.partial(fused_kernel, nodes, scale), out_shape=(...]
    pallas_call x0 -> x1, Pallas kernels: none -> 1.88 us  [publish_call(): pl.pallas_call(publish_kernel, out_shape=tuple((jax.ShapeDtypeStruct(a.sh...]
where the time goes in v2:
time: 84.9 us; the launch traced here: 84.5 us
  Pallas kernels  83.9 us (99%)
    pallas_call x1, Pallas kernels, fused_call(): pl.pallas_call(functools.partial(fused_kernel, nodes, scale), out_shape=(...  78.4 us
    pallas_call x1, Pallas kernels, table_call(): pl.pallas_call(functools.partial(table_kernel, capacity), out_shape=jax.S...  3.55 us
    pallas_call x1, Pallas kernels, publish_call(): pl.pallas_call(publish_kernel, out_shape=tuple((jax.ShapeDtypeStruct(a.sh...  1.88 us

profile of v2, /device:TPU:0, one launch (start us, length us, event | category | flops | bytes accessed | tf_op | source)
XLA Modules:
  0.0 84.5 jit_solution(14706541302315628070)
XLA Ops:
  0.6 3.5 %shard_map.103.table = s32[32,128]{1,0:T(8,128)} custom-call(s32[1,4]{1,0:T(1,128)} %bitcast.9, s32[4,96]{1,0:T(4,128)} %bitcast.7, s32[4,96]{1,0:T(4,128)} %bitcast.8), custom_call_target="tpu_custom_call" | custom-call | tf_op jit(solution)/shard_map/pallas_call | solution.py:72
  4.2 78.4 %shard_map.104 = (bf16[512,256]{1,0:T(8,128)(2,1)}, bf16[512,256]{1,0:T(8,128)(2,1)}, f32[256,256]{1,0:T(8,128)}) custom-call(s32[32,128]{1,0:T(8,128)} %shard_map.103.table, bf16[4,96,128,128]{3,2,1,0:T(8,128)(2,1)} %bitcast.5, bf16[2048,256]{1,0:T(8,128)(2,1)} %feature_src.1, s32[16,128]{1,0:T(8,128)} %bitcast.6, bf16[512,256]{1,0:T(8,128)(2,1)} %cot_src.1, ...), custom_call_target="tpu_custom_call" | custom-call | tf_op jit(solution)/shard_map/pallas_call | solution.py:530
  82.6 1.9 %shard_map.105 = (bf16[512,256]{1,0:T(8,128)(2,1)}, bf16[512,256]{1,0:T(8,128)(2,1)}, f32[256,256]{1,0:T(8,128)}) custom-call(bf16[512,256]{1,0:T(8,128)(2,1)} %get-tuple-element.6.refs_0_, bf16[512,256]{1,0:T(8,128)(2,1)} %get-tuple-element.7.refs_1_, f32[256,256]{1,0:T(8,128)} %get-tuple-element.8.refs_2_), custom_call_target="tpu_custom_call" | custom-call | tf_op jit(solution)/shard_map/pallas_call | solution.py:581

commit v3 on v2

--- a/solution.py
+++ b/solution.py
@@ -18,71 +18,40 @@
 BF16 = jnp.bfloat16
 
 
-def table_kernel(capacity, count_src, row_src, col_src, out, stage, count_ref, rows, cols, sems):
-    copies = [
-        pltpu.make_async_copy(src, dst, sems.at[i])
-        for i, (src, dst) in enumerate(((count_src, count_ref), (row_src, rows), (col_src, cols)))
-    ]
-    for copy in copies:
-        copy.start()
-    for copy in copies:
-        copy.wait()
+def sort_slots(capacity, count_ref, rows, cols, out, stage):
     lanes = stage.shape[1]
+    zero = jnp.int32(0)
     stage[...] = jnp.zeros_like(stage)
-    stage[0:4, 0:capacity] = rows[...].astype(F32)
-    stage[4:8, 0:capacity] = cols[...].astype(F32)
+    stage[0:4, 0:capacity] = rows[...]
+    stage[4:8, 0:capacity] = cols[...]
     by_slot = stage[...].T
-    sub = lax.broadcasted_iota(jnp.int32, (lanes, lanes), 0)
-    lane = lax.broadcasted_iota(jnp.int32, (lanes, lanes), 1)
-    lane_f = lane.astype(F32)
-    before = (lane < sub).astype(BF16)
-    upper = (sub < lane).astype(BF16)
-    head = lax.broadcasted_iota(jnp.int32, (8, lanes), 0)
+    sub = lax.broadcasted_iota(jnp.int32, (capacity, lanes), 0)
+    lane = lax.broadcasted_iota(jnp.int32, (capacity, lanes), 1)
     for way in range(2):
         for k in range(4):
-            key = by_slot[:, way * 4 + k : way * 4 + k + 1]
+            at, pick = (way * 4 + k) * FIELDS, way * 4 + k
+            key = by_slot[0:capacity, pick : pick + 1]
+            other = by_slot[0:capacity, (1 - way) * 4 + k : (1 - way) * 4 + k + 1]
+            along = stage[pick : pick + 1, :]
             live = sub < count_ref[0, k]
-            mine = jnp.where(live & (key == lane_f), 1.0, 0.0)
-            ahead = jnp.dot(before, mine.astype(BF16), preferred_element_type=F32)
-            held = jnp.sum(mine, axis=0, keepdims=True)
-            pairs = jnp.floor((held + 1.0) * 0.5)
-            base = jnp.dot(
-                jnp.broadcast_to(pairs, (8, lanes)).astype(BF16), upper, preferred_element_type=F32
-            )[0:1]
-            rank = jnp.sum(mine * ahead, axis=1, keepdims=True)
-            spot = jnp.sum(mine * (2.0 * base), axis=1, keepdims=True) + rank
-            put = jnp.where(live & (spot == lane_f), 1.0, 0.0)
-            starts = jnp.sum(jnp.where(rank == 0.0, put, 0.0), axis=0, keepdims=True)
-            other = stage[(1 - way) * 4 + k : (1 - way) * 4 + k + 1, :]
-            values = jnp.where(
-                head == 0, lane_f[0:8], jnp.where(head == 1, jnp.broadcast_to(other, (8, lanes)), 1.0)
-            )
-            found = jnp.dot(values.astype(BF16), put.astype(BF16), preferred_element_type=F32)
-            slot = jnp.where(found[2:3] > 0.0, found[0:1], float(capacity))
-            last = jnp.where(held > 0.0, base + pairs, 0.0)
-            at = (way * 4 + k) * FIELDS
-            out[at : at + 1, :] = slot.astype(jnp.int32)
-            out[at + 1 : at + 2, :] = found[1:2].astype(jnp.int32)
-            out[at + 2 : at + 3, :] = (1.0 - starts).astype(jnp.int32)
-            out[at + 3 : at + 4, :] = last.astype(jnp.int32)
-
-
-def table_call(counts, row_ids, col_ids):
-    capacity = row_ids.shape[-1]
-    return pl.pallas_call(
-        functools.partial(table_kernel, capacity),
-        out_shape=jax.ShapeDtypeStruct((8 * FIELDS, 128), jnp.int32),
-        in_specs=[pl.BlockSpec(memory_space=pl.ANY)] * 3,
-        out_specs=pl.BlockSpec(memory_space=pltpu.VMEM),
-        scratch_shapes=[
-            pltpu.VMEM((128, 128), F32),
-            pltpu.SMEM(counts.shape, jnp.int32),
-            pltpu.VMEM(row_ids.shape, jnp.int32),
-            pltpu.VMEM(col_ids.shape, jnp.int32),
-            pltpu.SemaphoreType.DMA((3,)),
-        ],
-        compiler_params=pltpu.CompilerParams(vmem_limit_bytes=VLIM * 1024 * 1024),
-    )(counts, row_ids, col_ids)
+            same = live & (key == along) & (lane < sub)
+            rank = jnp.sum(jnp.where(same, 1, zero), axis=1, keepdims=True)
+            held = jnp.sum(jnp.where(live & (key == lane), 1, zero), axis=0, keepdims=True)
+            odd = held - 2 * lax.shift_right_logical(held, 1)
+            padded = held + odd
+            base = jnp.sum(jnp.where(lane < key, padded, zero), axis=1, keepdims=True)
+            length = jnp.sum(jnp.where(lane == key, padded, zero), axis=1, keepdims=True)
+            spot = base + rank
+            put = live & (spot == lane)
+            slot = jnp.sum(jnp.where(put, sub - capacity, zero), axis=0, keepdims=True)
+            source = jnp.sum(jnp.where(put, other, zero), axis=0, keepdims=True)
+            starts = jnp.sum(jnp.where(put & (rank == 0), 1, zero), axis=0, keepdims=True)
+            reach = jnp.where(live & (key == lane) & (rank == 0), base + length, zero)
+            last = lax.shift_right_logical(jnp.sum(reach, axis=0, keepdims=True), 1)
+            out[at : at + 1, :] = slot + capacity
+            out[at + 1 : at + 2, :] = source
+            out[at + 2 : at + 3, :] = 1 - starts
+            out[at + 3 : at + 4, :] = last
 
 
 class Wires:
@@ -108,12 +77,12 @@
 
 
 def fused_kernel(
-    nodes, scale, table, tiles, feature_src, order_src, cot_src, weight_src,
-    act, grad, wgrad, features, order, cot, weight,
+    nodes, scale, count_src, row_src, col_src, tiles, feature_src, order_src, cot_src, weight_src,
+    act, grad, wgrad, count_ref, row_ids, col_ids, features, order, cot, weight,
     held, here, halo_a, halo_b, halo_c, sums, acc, part, near, outgoing, far, agg, pg, full,
     terms, tnear, tout, tfar, leaving, got, lleave, lgot, total, lout, lfar,
     wmine, wnear, wout, wfar, wstep, wgot, wfull, pick,
-    load_sems, stage_sems, send, recv,
+    stage, sorted_slots, table, load_sems, stage_sems, send, recv,
 ):
     capacity = tiles.shape[1]
     count, size, feat = here.shape
@@ -146,7 +115,8 @@
         pltpu.make_async_copy(src, dst, stage_sems.at[i])
         for i, (src, dst) in enumerate(
             (
-                (order_src, order), (feature_src, features), (cot_src, cot), (weight_src, weight),
+                (order_src, order), (feature_src, features), (count_src, count_ref),
+                (row_src, row_ids), (col_src, col_ids), (cot_src, cot), (weight_src, weight),
             )
         )
     ]
@@ -204,6 +174,9 @@
         reorder(2 * EXCL + SHARED * (1 - c) + i)
     for copy in staged[2:]:
         copy.wait()
+    sort_slots(capacity, count_ref, row_ids, col_ids, sorted_slots, stage)
+    fetch = pltpu.make_async_copy(sorted_slots, table, load_sems.at[4])
+    fetch.start()
     for k in range(4):
         held[k, capacity] = jnp.zeros((size, size), BF16)
     sums[0] = jnp.zeros((size, feat), F32)
@@ -284,6 +257,7 @@
     X = lambda g: (lambda: event_cross(g))
     S = lambda j: (lambda: event_shared(j))
 
+    fetch.wait()
     for load in loads:
         load.wait()
     sweep(0, 1, here, [[E(0)], [E(1)], [E(2), X(0)], [E(3), X(1)]])
@@ -507,7 +481,7 @@
     ).astype(grad.dtype)
 
 
-def fused_call(nodes, scale, table, tiles, features, order, cot, weight):
+def fused_call(nodes, scale, counts, row_ids, col_ids, tiles, features, order, cot, weight):
     capacity, size = tiles.shape[1], tiles.shape[-1]
     feat = features.shape[1]
     count = features.shape[0] // size
@@ -534,9 +508,12 @@
             jax.ShapeDtypeStruct(cot.shape, BF16),
             jax.ShapeDtypeStruct((feat, feat), F32),
         ),
-        in_specs=[pl.BlockSpec(memory_space=pltpu.SMEM)] + [pl.BlockSpec(memory_space=pl.ANY)] * 5,
+        in_specs=[pl.BlockSpec(memory_space=pltpu.MemorySpace.HBM)] * 8,
         out_specs=(vmem,) * 3,
         scratch_shapes=[
+            pltpu.SMEM(counts.shape, jnp.int32),
+            pltpu.VMEM(row_ids.shape, jnp.int32),
+            pltpu.VMEM(col_ids.shape, jnp.int32),
             pltpu.VMEM(features.shape, BF16),
             pltpu.VMEM(order.shape, jnp.int32),
             pltpu.VMEM(cot.shape, BF16),
@@ -550,15 +527,18 @@
             sums(tq + late), rows(late), rows(late),
             wide(4), wide(2), wide(), wide(), wide(steps), wide(steps), wide(4),
             pltpu.VMEM((tq * size, tq * size), BF16),
-            pltpu.SemaphoreType.DMA((4,)),
-            pltpu.SemaphoreType.DMA((4,)),
+            pltpu.VMEM((128, 128), jnp.int32),
+            pltpu.VMEM((8 * FIELDS, 128), jnp.int32),
+            pltpu.SMEM((8 * FIELDS, 128), jnp.int32),
+            pltpu.SemaphoreType.DMA((5,)),
+            pltpu.SemaphoreType.DMA((7,)),
             pltpu.SemaphoreType.DMA((128,)),
             pltpu.SemaphoreType.DMA((128,)),
         ],
         compiler_params=pltpu.CompilerParams(
             collective_id=0, has_side_effects=True, vmem_limit_bytes=VLIM * 1024 * 1024
         ),
-    )(table, tiles, features, order, cot, weight)
+    )(counts, row_ids, col_ids, tiles, features, order, cot, weight)
 
 
 def publish_kernel(*refs):
@@ -593,9 +573,9 @@
     nodes = lax.axis_size("node")
     size = tiles.shape[-1]
     scale = 1.0 / math.sqrt(features.shape[0] * nodes)
-    table = table_call(tile_count[0], tile_rows[0, 0], tile_cols[0, 0])
     outs = fused_call(
-        nodes, scale, table, tiles[0, 0], features, order.reshape(-1, size), cotangent, weight
+        nodes, scale, tile_count[0], tile_rows[0, 0], tile_cols[0, 0], tiles[0, 0],
+        features, order.reshape(-1, size), cotangent, weight,
     )
     return publish_call(*outs)
 

time: 84.9 us -> 79.6 us (0.938)
  Pallas kernels: 83.9 us -> 78.7 us
    pallas_call x1 -> x0, Pallas kernels: 3.55 us -> none  [table_call(): pl.pallas_call(functools.partial(table_kernel, capacity), out_shape=jax.S...]
    pallas_call x1, Pallas kernels: 78.4 us -> 76.9 us  [fused_call(): pl.pallas_call(functools.partial(fused_kernel, nodes, scale), out_shape=(...]
where the time goes in v3:
time: 79.6 us; the launch traced here: 79.4 us
  Pallas kernels  78.7 us (99%)
    pallas_call x1, Pallas kernels, fused_call(): pl.pallas_call(functools.partial(fused_kernel, nodes, scale), out_shape=(...  76.9 us
    pallas_call x1, Pallas kernels, publish_call(): pl.pallas_call(publish_kernel, out_shape=tuple((jax.ShapeDtypeStruct(a.sh...  1.88 us

profile of v3, /device:TPU:0, one launch (start us, length us, event | category | flops | bytes accessed | tf_op | source)
XLA Modules:
  0.0 79.4 jit_solution(10503157731083144884)
XLA Ops:
  0.6 76.9 %shard_map.103 = (bf16[512,256]{1,0:T(8,128)(2,1)}, bf16[512,256]{1,0:T(8,128)(2,1)}, f32[256,256]{1,0:T(8,128)}) custom-call(s32[1,4]{1,0:T(1,128)} %bitcast.9, s32[4,96]{1,0:T(4,128)} %bitcast.7, s32[4,96]{1,0:T(4,128)} %bitcast.8, bf16[4,96,128,128]{3,2,1,0:T(8,128)(2,1)} %bitcast.5, bf16[2048,256]{1,0:T(8,128)(2,1)} %feature_src.1, s32[16,128]{1,0:T(8,128)} %bitcast.6, ...), custom_call_target="tpu_custom_call" | custom-call | tf_op jit(solution)/shard_map/pallas_call | solution.py:504
  77.5 1.9 %shard_map.104 = (bf16[512,256]{1,0:T(8,128)(2,1)}, bf16[512,256]{1,0:T(8,128)(2,1)}, f32[256,256]{1,0:T(8,128)}) custom-call(bf16[512,256]{1,0:T(8,128)(2,1)} %get-tuple-element.6.refs_0_, bf16[512,256]{1,0:T(8,128)(2,1)} %get-tuple-element.7.refs_1_, f32[256,256]{1,0:T(8,128)} %get-tuple-element.8.refs_2_), custom_call_target="tpu_custom_call" | custom-call | tf_op jit(solution)/shard_map/pallas_call | solution.py:561

commit v4 on v3

--- a/solution.py
+++ b/solution.py
@@ -10,7 +10,7 @@
 
 EXCL = 3
 SHARED = 2
-EARLY = 3
+EARLY = 2
 GROUP = 14
 VLIM = 60
 FIELDS = 4
@@ -440,7 +440,7 @@
     terms_out(0)
     sweep(1, 2, full, [[], [C(*leg[0])], [W(1)], []])
     terms_out(2)
-    sweep(1, 1, full, [[L(*leg[3], 0)], [C(*leg[2]), L(*leg[3], 1)], [W(2), L(*leg[3], 2)], []])
+    sweep(1, 1, full, [[L(*leg[3], 0)], [C(*leg[2]), L(*leg[3], 1)], [W(2)], []])
     terms_out(1)
     terms_leave(*leg[0], 0)
     terms_cross(*leg[1])

time: 79.6 us -> 81.4 us (1.023)
  Pallas kernels: 78.7 us -> 80.6 us
    pallas_call x1, Pallas kernels: 76.9 us -> 78.7 us  [fused_call(): pl.pallas_call(functools.partial(fused_kernel, nodes, scale), out_shape=(...]
where the time goes in v4:
time: 81.4 us; the launch traced here: 81.2 us
  Pallas kernels  80.6 us (99%)
    pallas_call x1, Pallas kernels, fused_call(): pl.pallas_call(functools.partial(fused_kernel, nodes, scale), out_shape=(...  78.7 us
    pallas_call x1, Pallas kernels, publish_call(): pl.pallas_call(publish_kernel, out_shape=tuple((jax.ShapeDtypeStruct(a.sh...  1.88 us

profile of v4, /device:TPU:0, one launch (start us, length us, event | category | flops | bytes accessed | tf_op | source)
XLA Modules:
  0.0 81.2 jit_solution(14772571357727933665)
XLA Ops:
  0.6 78.7 %shard_map.103 = (bf16[512,256]{1,0:T(8,128)(2,1)}, bf16[512,256]{1,0:T(8,128)(2,1)}, f32[256,256]{1,0:T(8,128)}) custom-call(s32[1,4]{1,0:T(1,128)} %bitcast.9, s32[4,96]{1,0:T(4,128)} %bitcast.7, s32[4,96]{1,0:T(4,128)} %bitcast.8, bf16[4,96,128,128]{3,2,1,0:T(8,128)(2,1)} %bitcast.5, bf16[2048,256]{1,0:T(8,128)(2,1)} %feature_src.1, s32[16,128]{1,0:T(8,128)} %bitcast.6, ...), custom_call_target="tpu_custom_call" | custom-call | tf_op jit(solution)/shard_map/pallas_call | solution.py:504
  79.3 1.9 %shard_map.104 = (bf16[512,256]{1,0:T(8,128)(2,1)}, bf16[512,256]{1,0:T(8,128)(2,1)}, f32[256,256]{1,0:T(8,128)}) custom-call(bf16[512,256]{1,0:T(8,128)(2,1)} %get-tuple-element.6.refs_0_, bf16[512,256]{1,0:T(8,128)(2,1)} %get-tuple-element.7.refs_1_, f32[256,256]{1,0:T(8,128)} %get-tuple-element.8.refs_2_), custom_call_target="tpu_custom_call" | custom-call | tf_op jit(solution)/shard_map/pallas_call | solution.py:561
